TPU v7x, 32 devices: a whole 2x2x4 slice. The times are simulated.
32 devices in a mesh: pair: 8 (over z, y), aux: 4 (over x, core).
Axes of the slice: x: 2, y: 2, z: 4, core: 2. Of those that a mesh axis runs over, the one named last changes fastest.
Arguments:
- amplitudes: float32 [896, 8, 896], P('aux', 'pair'), may hold values from -6 to 6
- fitting: float32 [4, 896, 896], P('aux', 'pair'), may hold values from -0.09375 to 0.09375
Outputs:
- ladder: float32 [896, 8, 896], P('aux', 'pair')
All inputs are finite; a program needn't handle non-finite values.
Results may differ from a plain program's by a relative error of at most 0.0001.
Values sent between devices are 32-bit elements; how exact they have to be, the bound alone decides.
A program may use at most 64 MiB of HBM per device.

v0:
```python
import jax
import jax.numpy as jnp
from jax import lax
from jax.sharding import PartitionSpec as P


def per_device(amplitudes, fitting):
    width = amplitudes.shape[2]
    pair_dev = amplitudes.shape[1]
    count_fit = fitting.shape[0]
    whole_fit = lax.all_gather(fitting, "pair", axis=1, tiled=True)
    whole_amp = lax.all_gather(amplitudes, "aux", axis=0, tiled=True)
    halves = jnp.einsum(
        "rpd,lbd->lrpb",
        whole_amp,
        whole_fit,
        precision=lax.Precision.HIGHEST,
        preferred_element_type=jnp.float32,
    )
    halves = halves.reshape(count_fit, width, pair_dev * width)
    result = lax.psum_scatter(
        jnp.einsum(
            "lac,lcx->ax",
            whole_fit,
            halves,
            precision=lax.Precision.HIGHEST,
            preferred_element_type=jnp.float32,
        ),
        "aux",
        scatter_dimension=0,
        tiled=True,
    )
    return result.reshape(result.shape[0], pair_dev, width)


def solution(mesh):
    in_specs = (P("aux", "pair", None), P("aux", "pair", None))
    out_specs = P("aux", "pair", None)
    return jax.shard_map(
        per_device, mesh=mesh, in_specs=in_specs, out_specs=out_specs, check_vma=False
    )
```

profile of v0, /device:TPU:0, one launch (start us, length us, event | category | flops | bytes accessed | tf_op | source)
XLA Modules:
  0.0 180.0 jit_solution(6608431639948401352)
XLA Ops:
  6.5 0.0 all-gather.5.cloned.1.call-start
  6.5 0.7 all-gather.5.cloned.1.call-update
  7.3 0.0 all-gather.3.cloned.1.call-start
  7.3 0.7 all-gather.3.cloned.1.call-update
  8.0 0.0 reduce-scatter.4.cloned.1.call-start
  8.1 32.5 %all-gather.5.cloned.1.call-done = f32[896,1,896]{2,1,0:T(1,128)} async-done(((f32[224,1,896]{2,1,0:T(1,128)}), f32[896,1,896]{2,1,0:T(1,128)}) %all-gather.5.cloned.1.call-update) | async-done | bytes 3211280 | tf_op jit(solution)/shard_map/all_gather | solution.py:12
  40.5 62.9 %all-gather.3.cloned.1.call-done = f32[1,896,896]{2,1,0:T(8,128)} async-done(((f32[1,112,896]{2,1,0:T(8,128)}), f32[1,896,896]{2,1,0:T(8,128)}) %all-gather.3.cloned.1.call-update) | async-done | bytes 3211280 | tf_op jit(solution)/shard_map/all_gather | solution.py:11
  103.4 0.0 copy-start
  103.4 14.9 %fusion = f32[896,896]{1,0:T(8,128)S(1)} fusion(f32[896,1,896]{2,1,0:T(1,128)} %all-gather.5.cloned.1.call-done, f32[1,896,896]{2,1,0:T(8,128)} %all-gather.3.cloned.1.call-done), kind=kOutput, calls=%fused_computation | convolution fusion | flops 8631877632 | bytes 9633792 | tf_op jit(solution)/shard_map/rpd,lbd->lrpb/dot_general | solution.py:13
  118.3 0.0 copy-done
  118.3 11.7 %fusion.7 = f32[896,896]{0,1:T(8,128)S(1)} fusion(f32[1,896,896]{2,1,0:T(8,128)S(1)} %copy-done, f32[896,896]{1,0:T(8,128)S(1)} %fusion), kind=kOutput, calls=%fused_computation.7 | convolution fusion | flops 8631877632 | bytes 9633792 | tf_op jit(solution)/shard_map/lac,lcx->ax/dot_general | solution.py:22
  129.9 3.0 %copy.5 = f32[896,896]{1,0:T(8,128)} copy(f32[896,896]{0,1:T(8,128)S(1)} %fusion.7) | data formatting | bytes 6422528
  133.0 0.0 reduce-scatter.4.cloned.1.call-update
  133.0 37.1 %reduce-scatter.4.cloned.1.call-done = f32[224,896]{1,0:T(8,128)} async-done(((f32[896,896]{1,0:T(8,128)}), f32[224,896]{1,0:T(8,128)}) %reduce-scatter.4.cloned.1.call-update) | async-done | bytes 802832
  170.1 1.4 copy.6
  171.5 1.9 %copy.4 = f32[224,1,896]{2,1,0:T(1,128)} copy(f32[224,1,896]{0,2,1:T(8,128)S(1)} %bitcast.23) | data formatting | bytes 1605632 | tf_op jit(solution)/shard_map/reshape | solution.py:33
Async XLA Ops:
  6.5 34.0 %all-gather.5.cloned.1.call-start = ((), (), s32[]{:S(2)}) async-start(), calls=%async_computation.2 | async-start | bytes 4014080 | tf_op jit(solution)/shard_map/all_gather | solution.py:12
  7.3 96.2 %all-gather.3.cloned.1.call-start = ((), (), s32[]{:S(2)}) async-start(), calls=%async_computation.1 | async-start | bytes 3612672 | tf_op jit(solution)/shard_map/all_gather | solution.py:11
  8.0 162.1 %reduce-scatter.4.cloned.1.call-start = ((), (), s32[]{:S(2)}) async-start(), calls=%async_computation.3 | async-start | bytes 4014080
  103.4 14.9 %copy-start = (f32[1,896,896]{2,1,0:T(8,128)S(1)}, f32[1,896,896]{2,1,0:T(8,128)}, u32[]{:S(2)}) copy-start(f32[1,896,896]{2,1,0:T(8,128)} %all-gather.3.cloned.1.call-done) | copy-start | bytes 9633796
Sparse Core Ops, SparseCore 0:
  8.9 31.5 all-gather.4
  42.7 60.6 all-gather.2
  133.1 36.9 reduce-scatter.3
where the time goes:
time: 180 us
  waiting for transfers between devices  134 us (74%)
  matrix products  26.5 us (15%)
  between operations  13.1 us (7%)
  local copies, waits for them, and re-layouts  6.39 us (4%)
    all_gather x1, waiting for transfers between devices, per_device(): whole_fit = lax.all_gather(fitting, 'pair', axis=1, tiled=True)  62.9 us
    unnamed x4, waiting for transfers between devices  38.5 us
    all_gather x1, waiting for transfers between devices, per_device(): whole_amp = lax.all_gather(amplitudes, 'aux', axis=0, tiled=True)  32.5 us
    dot_general x1, matrix products, per_device(): jnp.einsum('rpd,lbd->lrpb', whole_amp, whole_fit, precision=lax.Precision...  14.9 us
    dot_general x1, matrix products, per_device(): jnp.einsum('lac,lcx->ax', whole_fit, halves, precision=lax.Precision.HIGH...  11.7 us
    unnamed x4, local copies, waits for them, and re-layouts  4.45 us
  transfers between devices with their start and end apart: 3, of which 3 were waited for; matrix products, arithmetic and copies ran while one was open for 0% of the time, Pallas kernels for 0%

commit v1 on v0

--- a/solution.py
+++ b/solution.py
@@ -9,7 +9,10 @@
     pair_dev = amplitudes.shape[1]
     count_fit = fitting.shape[0]
     whole_fit = lax.all_gather(fitting, "pair", axis=1, tiled=True)
-    whole_amp = lax.all_gather(amplitudes, "aux", axis=0, tiled=True)
+    main = lax.all_to_all(
+        jnp.stack([amplitudes for _ in range(lax.psum(1, "aux"))], axis=0), "aux", 0, 0
+    )
+    whole_amp = jnp.concatenate(main, axis=0)
     halves = jnp.einsum(
         "rpd,lbd->lrpb",
         whole_amp,

time: 180 us -> 149 us (0.83)
  waiting for transfers between devices: 134 us -> 58.8 us
  blocking collectives: 0 us -> 41.6 us
  local copies, waits for them, and re-layouts: 6.39 us -> 9.43 us
    all_gather x1, waiting for transfers between devices: 62.9 us -> 20.9 us  [per_device(): whole_fit = lax.all_gather(fitting, 'pair', axis=1, tiled=True)]
    all_to_all x0 -> x1, blocking collectives: none -> 41.6 us  [per_device(): lax.all_to_all(jnp.stack([amplitudes for _ in range(lax.psum(1, 'aux'))],...]
    all_gather x1 -> x0, waiting for transfers between devices: 32.5 us -> none  [per_device(): whole_amp = lax.all_gather(amplitudes, 'aux', axis=0, tiled=True)]
    unnamed x4 -> x6, local copies, waits for them, and re-layouts: 4.45 us -> 5.83 us
    unnamed x4 -> x3, waiting for transfers between devices: 38.5 us -> 37.9 us
  transfers between devices with their start and end apart: 3 -> 2, of which waited for: 3 -> 2; matrix products, arithmetic and copies ran while one was open for 0% -> 2% of each run, Pallas kernels for 0% -> 0%
where the time goes in v1:
time: 149 us
  waiting for transfers between devices  58.8 us (39%)
  blocking collectives  41.6 us (28%)
  matrix products  25.5 us (17%)
  between operations  13.4 us (9%)
  local copies, waits for them, and re-layouts  9.43 us (6%)
    all_to_all x1, blocking collectives, per_device(): lax.all_to_all(jnp.stack([amplitudes for _ in range(lax.psum(1, 'aux'))],...  41.6 us
    unnamed x3, waiting for transfers between devices  37.9 us
    all_gather x1, waiting for transfers between devices, per_device(): whole_fit = lax.all_gather(fitting, 'pair', axis=1, tiled=True)  20.9 us
    dot_general x1, matrix products, per_device(): jnp.einsum('rpd,lbd->lrpb', whole_amp, whole_fit, precision=lax.Precision...  14 us
    dot_general x1, matrix products, per_device(): jnp.einsum('lac,lcx->ax', whole_fit, halves, precision=lax.Precision.HIGH...  11.5 us
    unnamed x6, local copies, waits for them, and re-layouts  5.83 us
  transfers between devices with their start and end apart: 2, of which 2 were waited for; matrix products, arithmetic and copies ran while one was open for 2% of the time, Pallas kernels for 0%

profile of v1, /device:TPU:0, one launch (start us, length us, event | category | flops | bytes accessed | tf_op | source)
XLA Modules:
  0.0 148.8 jit_solution(8494522418118383180)
XLA Ops:
  6.5 0.0 all-gather.2.cloned.1.call-start
  6.5 0.7 all-gather.2.cloned.1.call-update
  7.3 0.0 reduce-scatter.4.cloned.1.call-start
  7.3 1.2 copy.10
  8.5 1.7 %stack.2 = f32[4,224,1,896]{3,2,1,0:T(1,128)S(1)} broadcast(f32[224,896]{1,0:T(8,128)S(1)} %bitcast.27), dimensions={1,3} | broadcast | bytes 4014080 | tf_op jit(solution)/shard_map/stack | solution.py:13
  10.2 41.6 %all_to_all.5 = f32[4,224,1,896]{3,2,1,0:T(1,128)S(1)} all-to-all(f32[4,224,1,896]{3,2,1,0:T(1,128)S(1)} %stack.2), channel_id=1, replica_groups=mesh['pair'=8,'aux'=4] {'aux'}, dimensions={0} | all-to-all | bytes 6422528 | tf_op jit(solution)/shard_map/all_to_all | solution.py:12
  51.8 0.2 copy.8
  52.0 20.9 %all-gather.2.cloned.1.call-done = f32[1,896,896]{2,1,0:T(8,128)} async-done(((f32[1,112,896]{2,1,0:T(8,128)}), f32[1,896,896]{2,1,0:T(8,128)}) %all-gather.2.cloned.1.call-update) | async-done | bytes 3211280 | tf_op jit(solution)/shard_map/all_gather | solution.py:11
  72.9 0.0 copy-start
  72.9 14.0 %fusion.3 = f32[896,896]{1,0:T(8,128)S(1)} fusion(f32[896,896]{1,0:T(8,128)S(1)} %bitcast.25, f32[1,896,896]{2,1,0:T(8,128)} %all-gather.2.cloned.1.call-done), kind=kOutput, calls=%fused_computation.3 | convolution fusion | flops 8631877632 | bytes 9633792 | tf_op jit(solution)/shard_map/rpd,lbd->lrpb/dot_general | solution.py:16
  87.0 0.0 copy-done
  87.0 11.5 %fusion.5 = f32[896,896]{0,1:T(8,128)S(1)} fusion(f32[1,896,896]{2,1,0:T(8,128)S(1)} %copy-done, f32[896,896]{1,0:T(8,128)S(1)} %fusion.3), kind=kOutput, calls=%fused_computation.5 | convolution fusion | flops 8631877632 | bytes 9633792 | tf_op jit(solution)/shard_map/lac,lcx->ax/dot_general | solution.py:25
  98.4 3.0 %copy.5 = f32[896,896]{1,0:T(8,128)} copy(f32[896,896]{0,1:T(8,128)S(1)} %fusion.5) | data formatting | bytes 6422528
  101.4 0.0 reduce-scatter.4.cloned.1.call-update
  101.5 37.1 %reduce-scatter.4.cloned.1.call-done = f32[224,896]{1,0:T(8,128)} async-done(((f32[896,896]{1,0:T(8,128)}), f32[224,896]{1,0:T(8,128)}) %reduce-scatter.4.cloned.1.call-update) | async-done | bytes 802832
  138.6 1.4 copy.6
  140.0 1.9 %copy.4 = f32[224,1,896]{2,1,0:T(1,128)} copy(f32[224,1,896]{0,2,1:T(8,128)S(1)} %bitcast.26) | data formatting | bytes 1605632 | tf_op jit(solution)/shard_map/reshape | solution.py:36
Async XLA Ops:
  6.5 66.4 %all-gather.2.cloned.1.call-start = ((), (), s32[]{:S(2)}) async-start(), calls=%async_computation.2 | async-start | bytes 3612672 | tf_op jit(solution)/shard_map/all_gather | solution.py:11
  7.3 131.3 %reduce-scatter.4.cloned.1.call-start = ((), (), s32[]{:S(2)}) async-start(), calls=%async_computation.3 | async-start | bytes 4014080
  72.9 14.0 %copy-start = (f32[1,896,896]{2,1,0:T(8,128)S(1)}, f32[1,896,896]{2,1,0:T(8,128)}, u32[]{:S(2)}) copy-start(f32[1,896,896]{2,1,0:T(8,128)} %all-gather.2.cloned.1.call-done) | copy-start | bytes 9633796
Sparse Core Ops, SparseCore 0:
  9.5 63.3 all-gather.1
  101.6 36.9 reduce-scatter.3
